TPU v7x, 32 devices: a whole 2x2x4 slice. The times are simulated.
32 devices in a mesh: dp: 2 (over y), expert: 16 (over z, x, core).
Axes of the slice: x: 2, y: 2, z: 4, core: 2. Of those that a mesh axis runs over, the one named last changes fastest.
Arguments:
- tokens: bfloat16 [4096, 2048], P(('dp', 'expert')), may hold values from -6 to 6
- grad_out: bfloat16 [4096, 2048], P(('dp', 'expert')), may hold values from -6 to 6
- expert_ids: int32 [4096, 8], P(('dp', 'expert')), may hold values from 0 to 15, all different within a row; in each aligned block of 128 rows (0 to 127, 128 to 255, ...) at most 72 rows name the same one
- route_weight: bfloat16 [4096, 8], P(('dp', 'expert')), may hold values from 0.049804688 to 1
- w_gate: bfloat16 [16, 2048, 384], P('expert', 'dp'), may hold values from -0.125 to 0.125
- w_up: bfloat16 [16, 2048, 384], P('expert', 'dp'), may hold values from -0.125 to 0.125
- w_down: bfloat16 [16, 384, 2048], P('expert', None, 'dp'), may hold values from -0.3125 to 0.3125
Outputs:
- grad_tokens: bfloat16 [4096, 2048], P(('dp', 'expert'))
- grad_route: bfloat16 [4096, 8], P(('dp', 'expert'))
Inputs may be any that keep to these rules, and one draw needn't show every extreme that they name: `expert_ids`: each row names 8 different experts; among the 128 rows of one device no expert is named by more than 72 rows, and in every draw some expert is named by exactly 72 rows of some device.
All inputs are finite; a program needn't handle non-finite values.
Results may differ from a plain program's by a relative error of at most 0.012.
Values may be sent and summed in bfloat16 or wider, within the bound.
A program may use at most 128 MiB of HBM per device.

v0:
```python
import jax
import jax.numpy as jnp
from jax import lax
from jax.sharding import PartitionSpec as P


def expert_rows(x_rows, g_rows, weight_rows, gate_mat, up_mat, down_mat):
    gate_pre = jnp.dot(x_rows, gate_mat, preferred_element_type=jnp.float32)
    up_pre = jnp.dot(x_rows, up_mat, preferred_element_type=jnp.float32)
    sigmoid_gate = jax.nn.sigmoid(gate_pre)
    active = gate_pre * sigmoid_gate
    hidden = active * up_pre
    back_hidden = jnp.dot(g_rows, down_mat.T, preferred_element_type=jnp.float32)
    route_grad = jnp.sum(hidden * back_hidden, axis=1)
    scaled = weight_rows.astype(jnp.float32)[:, None] * back_hidden
    slope = sigmoid_gate * (1.0 + gate_pre * (1.0 - sigmoid_gate))
    d_gate = (scaled * up_pre * slope).astype(jnp.bfloat16)
    d_up = (scaled * active).astype(jnp.bfloat16)
    input_grad = jnp.dot(d_gate, gate_mat.T, preferred_element_type=jnp.float32) + jnp.dot(
        d_up, up_mat.T, preferred_element_type=jnp.float32
    )
    return (input_grad.astype(jnp.bfloat16), route_grad.astype(jnp.bfloat16))


def fetch_rows(tokens, grad_out, flat_weight, assign_of, top_k):
    token_of = assign_of // top_k
    rows_x = jnp.take(tokens, token_of, axis=0, mode="fill", fill_value=0)
    rows_g = jnp.take(grad_out, token_of, axis=0, mode="fill", fill_value=0)
    rows_w = jnp.take(flat_weight, assign_of, axis=0, mode="fill", fill_value=0)
    return (rows_x, rows_g, rows_w)


def per_device(tokens, grad_out, expert_ids, route_weight, w_gate, w_up, w_down):
    tok_rows, width_model = tokens.shape
    top_k = expert_ids.shape[1]
    n_assign = tok_rows * top_k
    n_expert = lax.axis_size("expert")
    capacity = 9 * tok_rows * top_k // (8 * n_expert)
    slots_all = n_expert * capacity
    gate_mat, up_mat, down_mat = (
        lax.all_gather(w_gate[0], "dp", axis=0, tiled=True),
        lax.all_gather(w_up[0], "dp", axis=0, tiled=True),
        lax.all_gather(w_down[0], "dp", axis=1, tiled=True),
    )
    flat_ids = expert_ids.reshape(-1)
    flat_weight = route_weight.reshape(-1)
    onehot = (flat_ids[:, None] == jnp.arange(n_expert, dtype=jnp.int32)[None, :]).astype(jnp.int32)
    earlier = jnp.cumsum(onehot, axis=0) - onehot
    slot_of = jnp.sum(earlier * onehot, axis=1)
    placed = flat_ids * capacity + slot_of
    assign_index = jnp.arange(n_assign, dtype=jnp.int32)
    slot_assign = (
        jnp.full((slots_all,), n_assign, jnp.int32).at[placed].set(assign_index, mode="drop")
    )
    send_x, send_g, send_w = fetch_rows(tokens, grad_out, flat_weight, slot_assign, top_k)
    send_x = send_x.reshape(n_expert, capacity, width_model)
    send_g = send_g.reshape(n_expert, capacity, width_model)
    send_w = send_w.reshape(n_expert, capacity)
    got_x, got_g, got_w = (
        lax.all_to_all(send_x, "expert", split_axis=0, concat_axis=0, tiled=True),
        lax.all_to_all(send_g, "expert", split_axis=0, concat_axis=0, tiled=True),
        lax.all_to_all(send_w, "expert", split_axis=0, concat_axis=0, tiled=True),
    )
    out_grad, out_route = expert_rows(
        got_x.reshape(slots_all, width_model),
        got_g.reshape(slots_all, width_model),
        got_w.reshape(slots_all),
        gate_mat,
        up_mat,
        down_mat,
    )
    out_grad = out_grad.reshape(n_expert, capacity, width_model)
    out_route = out_route.reshape(n_expert, capacity)
    back_grad, back_route = (
        lax.all_to_all(out_grad, "expert", split_axis=0, concat_axis=0, tiled=True),
        lax.all_to_all(out_route, "expert", split_axis=0, concat_axis=0, tiled=True),
    )
    part_flat = back_grad.reshape(slots_all, width_model)[placed]
    route_flat = back_route.reshape(slots_all)[placed]
    part_rows = part_flat.reshape(tok_rows, top_k, width_model)
    grad_tokens = jnp.sum(part_rows.astype(jnp.float32), axis=1).astype(jnp.bfloat16)
    grad_route = route_flat.reshape(tok_rows, top_k)
    return (grad_tokens, grad_route)


def solution(mesh):
    return jax.shard_map(
        per_device,
        mesh=mesh,
        in_specs=(
            P(("dp", "expert"), None),
            P(("dp", "expert"), None),
            P(("dp", "expert"), None),
            P(("dp", "expert"), None),
            P("expert", "dp", None),
            P("expert", "dp", None),
            P("expert", None, "dp"),
        ),
        out_specs=(P(("dp", "expert"), None), P(("dp", "expert"), None)),
        check_vma=False,
    )
```

profile of v0, /device:TPU:11, one launch (start us, length us, event | category | flops | bytes accessed | tf_op | source)
XLA Modules:
  0.0 429.3 jit_solution(9125871058928897859)
XLA Ops:
  7.2 0.0 copy-start
  7.2 0.7 broadcast_multiply_fusion
  7.9 0.8 copy.19
  8.7 0.1 eq.29
  8.8 0.1 eq.25
  8.9 0.8 copy.23
  9.7 0.1 reshape.140
  9.8 0.1 copy.18
  9.9 0.1 mul.53
  10.0 4.5 %reduce-window.6 = s32[16,8,128]{2,1,0:T(8,128)S(1)} reduce-window(s32[16,8,128]{2,1,0:T(8,128)S(1)} %fusion.18, s32[]{:T(128)} %constant.47.clone.1), window={size=1x1x128 pad=0_0x0_0x127_0}, to_apply=%region_0.0 | reduce-window | flops 2080768 | bytes 131076 | tf_op jit(solution)/shard_map/reduce-window
  14.5 0.1 slice.18
  14.6 0.1 copy.21
  14.8 0.1 copy.22
  14.9 0.1 broadcast_add_fusion
  15.0 4.3 %scatter_custom_fusion = s32[1152]{0:T(1024)S(1)} fusion(s32[1024]{0:T(1024)S(1)} %bitcast.55, s32[1024]{0:T(1024)S(1)} %iota.11, s32[]{:T(128)} %constant.31.clone.1), kind=kCustom, calls=%fused_computation.51 | custom fusion | bytes 4612 | tf_op jit(solution)/shard_map/scatter | solution.py:53
  19.4 7.3 %gather_fusion = bf16[1152]{0:T(1024)(128)(2,1)S(1)} fusion(bf16[1024]{0:T(1024)(128)(2,1)S(1)} %reshape.140, s32[2048]{0:T(1024)S(1)} %pad_clamp_fusion.1), kind=kCustom, calls=%fused_computation.2 | custom fusion | bytes 9216 | tf_op jit(solution)/shard_map/jit(_take)/gather | solution.py:29
  26.7 0.7 select_n.53
  27.4 6.5 %all-to-all-start = ((bf16[16,1,72]{2,1,0:T(2,128)(2,1)}), bf16[16,1,72]{2,1,0:T(2,128)(2,1)S(1)}, u32[]{:S(2)}, u32[]{:S(2)}) async-start(bf16[16,1,72]{2,1,0:T(2,128)(2,1)} %select_n.53), calls=%async_computation | async-start | bytes 16384 | tf_op jit(solution)/shard_map/all_to_all | solution.py:62
  33.9 0.0 copy-done
  33.9 0.0 copy-start.1
  33.9 5.9 %gather_fusion.4 = bf16[1152,2048]{1,0:T(8,128)(2,1)} fusion(bf16[128,2048]{1,0:T(8,128)(2,1)S(1)} %copy-done, s32[2048]{0:T(1024)S(1)} %pad_clamp_fusion), kind=kCustom, calls=%fused_computation.1.clone | custom fusion | bytes 9441792 | tf_op jit(solution)/shard_map/jit(_take)/gather | solution.py:27
  39.8 0.0 copy-done.1
  39.8 5.9 %gather_fusion.3 = bf16[1152,2048]{1,0:T(8,128)(2,1)} fusion(bf16[128,2048]{1,0:T(8,128)(2,1)S(1)} %copy-done.1, s32[2048]{0:T(1024)S(1)} %pad_clamp_fusion), kind=kCustom, calls=%fused_computation.clone | custom fusion | bytes 9441792 | tf_op jit(solution)/shard_map/jit(_take)/gather | solution.py:28
  45.8 8.5 %broadcast_select_fusion.1 = (bf16[1152,2048]{1,0:T(8,128)(2,1)}, bf16[1152,2048]{1,0:T(8,128)(2,1)}) fusion(bf16[1152,2048]{1,0:T(8,128)(2,1)} %gather_fusion.3, pred[1152]{0:T(1024)(128)(4,1)S(1)} %get-tuple-element.7, bf16[1152,2048]{1,0:T(8,128)(2,1)} %gather_fusion.4), kind=kLoop, calls=%fused_computation.9 | loop fusion | flops 4718592 | bytes 18875520 | tf_op jit(solution)/shard_map/jit(_take)/select_n | solution.py:28
  54.3 0.0 all-to-all-done
  54.3 109.6 %all_to_all.27 = bf16[16,72,2048]{2,1,0:T(8,128)(2,1)} all-to-all(bf16[16,72,2048]{2,1,0:T(8,128)(2,1)} %bitcast.48), channel_id=1, replica_groups=mesh['dp'=2,'expert'=16] {'expert'}, dimensions={0} | all-to-all | bytes 9437184 | tf_op jit(solution)/shard_map/all_to_all | solution.py:60
  163.8 5.3 %all-to-all-start.1 = ((bf16[16,72,2048]{2,1,0:T(8,128)(2,1)}), bf16[16,72,2048]{2,1,0:T(8,128)(2,1)}, u32[]{:S(2)}, u32[]{:S(2)}) async-start(bf16[16,72,2048]{2,1,0:T(8,128)(2,1)} %bitcast.47), calls=%async_computation.1 | async-start | bytes 9437184 | tf_op jit(solution)/shard_map/all_to_all | solution.py:61
  169.1 0.0 all-gather.11.cloned.1.call-start
  169.1 0.7 all-gather.11.cloned.1.call-update
  169.8 0.0 all-gather.9.cloned.1.call-start
  169.9 0.7 all-gather.9.cloned.1.call-update
  170.6 0.2 all-gather.7.cloned.1.call-start
  170.8 0.5 all-gather.7.cloned.1.call-update
  171.3 0.1 reshape.150
  171.4 27.7 %all-gather.11.cloned.1.call-done = bf16[1,2048,384]{2,1,0:T(8,128)(2,1)} async-done(((bf16[1,1024,384]{2,1,0:T(8,128)(2,1)}), bf16[1,2048,384]{2,1,0:T(8,128)(2,1)}) %all-gather.11.cloned.1.call-update) | async-done | bytes 1572880 | tf_op jit(solution)/shard_map/all_gather | solution.py:41
  199.1 5.1 %fusion.4 = f32[1152,384]{0,1:T(8,128)S(1)} fusion(bf16[1152,2048]{1,0:T(8,128)(2,1)} %bitcast.50, bf16[1,2048,384]{2,1,0:T(8,128)(2,1)} %all-gather.11.cloned.1.call-done), kind=kOutput, calls=%fused_computation.18 | convolution fusion | flops 1811939328 | bytes 8060928 | tf_op jit(solution)/shard_map/dot_general | solution.py:8
  204.2 23.7 %all-gather.9.cloned.1.call-done = bf16[1,2048,384]{2,1,0:T(8,128)(2,1)} async-done(((bf16[1,1024,384]{2,1,0:T(8,128)(2,1)}), bf16[1,2048,384]{2,1,0:T(8,128)(2,1)}) %all-gather.9.cloned.1.call-update) | async-done | bytes 1572880 | tf_op jit(solution)/shard_map/all_gather | solution.py:42
  227.9 6.3 %fusion.7 = f32[1152,384]{0,1:T(8,128)} fusion(bf16[1152,2048]{1,0:T(8,128)(2,1)} %bitcast.51, bf16[1,2048,384]{2,1,0:T(8,128)(2,1)} %all-gather.9.cloned.1.call-done), kind=kOutput, calls=%fused_computation.21 | convolution fusion | flops 1811939328 | bytes 8060928 | tf_op jit(solution)/shard_map/dot_general | solution.py:9
  234.2 22.5 %all-gather.7.cloned.1.call-done = bf16[1,384,2048]{2,1,0:T(8,128)(2,1)} async-done(((bf16[1,384,1024]{2,1,0:T(8,128)(2,1)}), bf16[1,384,2048]{2,1,0:T(8,128)(2,1)}) %all-gather.7.cloned.1.call-update) | async-done | bytes 1572880 | tf_op jit(solution)/shard_map/all_gather | solution.py:43
  256.7 16.1 %all-to-all-done.1 = bf16[16,72,2048]{2,1,0:T(8,128)(2,1)} async-done(((bf16[16,72,2048]{2,1,0:T(8,128)(2,1)}), bf16[16,72,2048]{2,1,0:T(8,128)(2,1)}, u32[]{:S(2)}, u32[]{:S(2)}) %all-to-all-start.1) | async-done | bytes 4718624 | tf_op jit(solution)/shard_map/all_to_all | solution.py:61
  272.8 6.8 %multiply_reduce_fusion = (bf16[1152]{0:T(1024)(128)(2,1)S(1)}, f32[1152,384]{0,1:T(8,128)}) fusion(f32[1152,384]{0,1:T(8,128)} %fusion.7, f32[1152,384]{0,1:T(8,128)S(1)} %fusion.4, bf16[1152,2048]{1,0:T(8,128)(2,1)} %bitcast.5, bf16[1,384,2048]{2,1,0:T(8,128)(2,1)} %all-gather.7.cloned.1.call-done), kind=kOutput, calls=%fused_computation.11 | convolution fusion | flops 1815034752 | bytes 11602176 | tf_op jit(solution)/shard_map/dot_general | solution.py:13
  279.6 0.7 convert_element_type.52
  280.3 4.8 %all-to-all-start.4 = ((bf16[16,1,72]{2,1,0:T(2,128)(2,1)}), bf16[16,1,72]{2,1,0:T(2,128)(2,1)S(1)}, u32[]{:S(2)}, u32[]{:S(2)}) async-start(bf16[16,1,72]{2,1,0:T(2,128)(2,1)} %convert_element_type.52), calls=%async_computation.4 | async-start | bytes 16384 | tf_op jit(solution)/shard_map/all_to_all | solution.py:76
  285.1 0.0 copy-start.2
  285.1 0.0 copy-start.3
  285.1 5.6 %fusion.2 = f32[1152,2048]{1,0:T(8,128)S(1)} fusion(bf16[1,2048,384]{2,1,0:T(8,128)(2,1)} %all-gather.11.cloned.1.call-done, f32[1152,384]{0,1:T(8,128)S(1)} %fusion.4, f32[1152,384]{0,1:T(8,128)} %fusion.7, f32[1152,384]{0,1:T(8,128)} %get-tuple-element.12, f32[1152]{0:T(1024)S(1)} %reshape.150), kind=kOutput, calls=%fused_computation.16 | convolution fusion | flops 1816805376 | bytes 16323072 | tf_op jit(solution)/shard_map/dot_general | solution.py:19
  290.7 0.0 copy-done.2
  290.8 0.0 copy-done.3
  290.8 4.5 %fusion = bf16[1152,2048]{1,0:T(8,128)(2,1)} fusion(f32[1152,2048]{1,0:T(8,128)S(1)} %fusion.2, bf16[1,2048,384]{2,1,0:T(8,128)(2,1)S(1)} %copy-done.3, f32[1152,384]{0,1:T(8,128)S(1)} %copy-done.2, f32[1152]{0:T(1024)S(1)} %reshape.150, f32[1152,384]{0,1:T(8,128)S(1)} %fusion.4), kind=kOutput, calls=%fused_computation.7 | convolution fusion | flops 1819754496 | bytes 19272192 | tf_op jit(solution)/shard_map/dot_general | solution.py:19
  295.3 0.0 all-to-all-done.4
  295.3 6.0 %all-to-all-start.3 = ((bf16[16,72,2048]{2,1,0:T(8,128)(2,1)}), bf16[16,72,2048]{2,1,0:T(8,128)(2,1)}, u32[]{:S(2)}, u32[]{:S(2)}) async-start(bf16[16,72,2048]{2,1,0:T(8,128)(2,1)} %bitcast.49), calls=%async_computation.3 | async-start | bytes 9437184 | tf_op jit(solution)/shard_map/all_to_all | solution.py:75
  301.4 0.1 reshape.148
  301.5 6.8 %gather_fusion.2 = bf16[1024]{0:T(1024)(128)(2,1)S(1)} fusion(bf16[1152]{0:T(1024)(128)(2,1)S(1)} %reshape.148, s32[1024]{0:T(1024)S(1)} %broadcast_clamp_fusion), kind=kCustom, calls=%fused_computation.4 | custom fusion | bytes 8192 | tf_op jit(solution)/shard_map/gather | solution.py:79
  308.3 0.1 reshape.149
  308.4 0.7 copy.26
  309.1 96.0 %all-to-all-done.3 = bf16[16,72,2048]{2,1,0:T(8,128)(2,1)} async-done(((bf16[16,72,2048]{2,1,0:T(8,128)(2,1)}), bf16[16,72,2048]{2,1,0:T(8,128)(2,1)}, u32[]{:S(2)}, u32[]{:S(2)}) %all-to-all-start.3) | async-done | bytes 4718624 | tf_op jit(solution)/shard_map/all_to_all | solution.py:75
  405.0 11.8 %gather_fusion.1 = bf16[1024,2048]{1,0:T(8,128)(2,1)} fusion(bf16[1152,2048]{1,0:T(8,128)(2,1)} %bitcast.12, s32[1024]{0:T(1024)S(1)} %broadcast_clamp_fusion), kind=kCustom, calls=%fused_computation.3 | custom fusion | bytes 8392704 | tf_op jit(solution)/shard_map/gather | solution.py:78
  416.9 5.9 %bitcast_reduce_fusion = bf16[128,2048]{1,0:T(8,128)(2,1)} fusion(bf16[1024,2048]{1,0:T(8,128)(2,1)} %gather_fusion.1), kind=kLoop, calls=%fused_computation.10 | loop fusion | flops 1835008 | bytes 4718592 | tf_op jit(solution)/shard_map/reduce_sum | solution.py:81
  (14 shorter events, 0.2 us)
Async XLA Ops:
  7.2 26.7 %copy-start = (bf16[128,2048]{1,0:T(8,128)(2,1)S(1)}, bf16[128,2048]{1,0:T(8,128)(2,1)}, u32[]{:S(2)}) copy-start(bf16[128,2048]{1,0:T(8,128)(2,1)} %param.9) | copy-start | bytes 1572868
  27.4 26.9 %all-to-all-start = ((bf16[16,1,72]{2,1,0:T(2,128)(2,1)}), bf16[16,1,72]{2,1,0:T(2,128)(2,1)S(1)}, u32[]{:S(2)}, u32[]{:S(2)}) async-start(bf16[16,1,72]{2,1,0:T(2,128)(2,1)} %select_n.53), calls=%async_computation | async-start | bytes 16384 | tf_op jit(solution)/shard_map/all_to_all | solution.py:62
  33.9 5.9 %copy-start.1 = (bf16[128,2048]{1,0:T(8,128)(2,1)S(1)}, bf16[128,2048]{1,0:T(8,128)(2,1)}, u32[]{:S(2)}) copy-start(bf16[128,2048]{1,0:T(8,128)(2,1)} %param.10) | copy-start | bytes 1572868
  163.8 109.0 %all-to-all-start.1 = ((bf16[16,72,2048]{2,1,0:T(8,128)(2,1)}), bf16[16,72,2048]{2,1,0:T(8,128)(2,1)}, u32[]{:S(2)}, u32[]{:S(2)}) async-start(bf16[16,72,2048]{2,1,0:T(8,128)(2,1)} %bitcast.47), calls=%async_computation.1 | async-start | bytes 9437184 | tf_op jit(solution)/shard_map/all_to_all | solution.py:61
  169.1 30.0 %all-gather.11.cloned.1.call-start = ((), (), s32[]{:S(2)}) async-start(), calls=%async_computation.7 | async-start | bytes 2359296 | tf_op jit(solution)/shard_map/all_gather | solution.py:41
  169.8 58.1 %all-gather.9.cloned.1.call-start = ((), (), s32[]{:S(2)}) async-start(), calls=%async_computation.6 | async-start | bytes 2359296 | tf_op jit(solution)/shard_map/all_gather | solution.py:42
  170.6 86.1 %all-gather.7.cloned.1.call-start = ((), (), s32[]{:S(2)}) async-start(), calls=%async_computation.5 | async-start | bytes 2359296 | tf_op jit(solution)/shard_map/all_gather | solution.py:43
  280.3 15.0 %all-to-all-start.4 = ((bf16[16,1,72]{2,1,0:T(2,128)(2,1)}), bf16[16,1,72]{2,1,0:T(2,128)(2,1)S(1)}, u32[]{:S(2)}, u32[]{:S(2)}) async-start(bf16[16,1,72]{2,1,0:T(2,128)(2,1)} %convert_element_type.52), calls=%async_computation.4 | async-start | bytes 16384 | tf_op jit(solution)/shard_map/all_to_all | solution.py:76
  285.1 5.6 %copy-start.2 = (f32[1152,384]{0,1:T(8,128)S(1)}, f32[1152,384]{0,1:T(8,128)}, u32[]{:S(2)}) copy-start(f32[1152,384]{0,1:T(8,128)} %get-tuple-element.12) | copy-start | bytes 5308420
  285.1 5.6 %copy-start.3 = (bf16[1,2048,384]{2,1,0:T(8,128)(2,1)S(1)}, bf16[1,2048,384]{2,1,0:T(8,128)(2,1)}, u32[]{:S(2)}) copy-start(bf16[1,2048,384]{2,1,0:T(8,128)(2,1)} %all-gather.9.cloned.1.call-done) | copy-start | bytes 4718596
  295.3 109.7 %all-to-all-start.3 = ((bf16[16,72,2048]{2,1,0:T(8,128)(2,1)}), bf16[16,72,2048]{2,1,0:T(8,128)(2,1)}, u32[]{:S(2)}, u32[]{:S(2)}) async-start(bf16[16,72,2048]{2,1,0:T(8,128)(2,1)} %bitcast.49), calls=%async_computation.3 | async-start | bytes 9437184 | tf_op jit(solution)/shard_map/all_to_all | solution.py:75
Sparse Core Ops, SparseCore 0:
  171.4 27.6 all-gather.10
  200.7 27.1 all-gather.8
  229.4 27.1 all-gather.6
where the time goes:
time: 430 us; the launch traced here: 429 us
  waiting for transfers between devices  188 us (44%)
  blocking collectives  110 us (26%)
  local copies, waits for them, and re-layouts  46.7 us (11%)
  matrix products  28.4 us (7%)
  starting transfers between devices  22.9 us (5%)
  other arithmetic  19.9 us (5%)
  between operations  13.9 us (3%)
    all_to_all x1, blocking collectives, per_device(): lax.all_to_all(send_x, 'expert', split_axis=0, concat_axis=0, tiled=True)  110 us
    all_to_all x1, waiting for transfers between devices, per_device(): lax.all_to_all(out_grad, 'expert', split_axis=0, concat_axis=0, tiled=True)  96 us
    all_gather x1, waiting for transfers between devices, per_device(): lax.all_gather(w_gate[0], 'dp', axis=0, tiled=True)  27.7 us
    all_gather x1, waiting for transfers between devices, per_device(): lax.all_gather(w_up[0], 'dp', axis=0, tiled=True)  23.7 us
    all_gather x1, waiting for transfers between devices, per_device(): lax.all_gather(w_down[0], 'dp', axis=1, tiled=True)  22.5 us
    all_to_all x1, waiting for transfers between devices, per_device(): lax.all_to_all(send_g, 'expert', split_axis=0, concat_axis=0, tiled=True)  16.1 us
    gather x1, local copies, waits for them, and re-layouts, per_device(): part_flat = back_grad.reshape(slots_all, width_model)[placed]  11.8 us
  transfers between devices with their start and end apart: 7, of which 5 were waited for; matrix products, arithmetic and copies ran while one was open for 12% of the time, Pallas kernels for 0%

commit v1 on v0

--- a/solution.py
+++ b/solution.py
@@ -2,6 +2,28 @@
 import jax.numpy as jnp
 from jax import lax
 from jax.sharding import PartitionSpec as P
+
+
+def split_up(x, dim, size):
+    before, after = (x.shape[:dim], x.shape[dim + 1 :])
+    return jnp.moveaxis(x.reshape(*before, size, -1, *after), dim, 0)
+
+
+def joined_along(blocks, dim):
+    shape = list(blocks.shape[1:])
+    shape[dim] *= blocks.shape[0]
+    return jnp.moveaxis(blocks, 0, dim).reshape(shape)
+
+
+def pairwise_exchange(x, axis, split_dim, concat_dim):
+    size, index = (lax.axis_size(axis), lax.axis_index(axis))
+    tiles = split_up(x, split_dim, size)
+    outs = [tiles[index]]
+    for step in range(1, size):
+        sent = tiles[index ^ step]
+        outs.append(lax.ppermute(sent, axis, [(i, i ^ step) for i in range(size)]))
+    tiles = jnp.stack(outs)[index ^ jnp.arange(size)]
+    return joined_along(tiles, concat_dim)
 
 
 def expert_rows(x_rows, g_rows, weight_rows, gate_mat, up_mat, down_mat):
@@ -72,7 +94,7 @@
     out_grad = out_grad.reshape(n_expert, capacity, width_model)
     out_route = out_route.reshape(n_expert, capacity)
     back_grad, back_route = (
-        lax.all_to_all(out_grad, "expert", split_axis=0, concat_axis=0, tiled=True),
+        pairwise_exchange(out_grad, "expert", 0, 0),
         lax.all_to_all(out_route, "expert", split_axis=0, concat_axis=0, tiled=True),
     )
     part_flat = back_grad.reshape(slots_all, width_model)[placed]

time: 430 us -> 448 us (1.042)
  local copies, waits for them, and re-layouts: 46.7 us -> 69.6 us
  waiting for transfers between devices: 188 us -> 170 us
  starting transfers between devices: 22.9 us -> 39.8 us
    all_to_all x1 -> x0, waiting for transfers between devices: 96 us -> none  [per_device(): lax.all_to_all(out_grad, 'expert', split_axis=0, concat_axis=0, tiled=True)]
    ppermute x0 -> x15, waiting for transfers between devices: none -> 78.1 us  [pairwise_exchange(): outs.append(lax.ppermute(sent, axis, [(i, i ^ step) for i in range(size)]))]
    ppermute x0 -> x15, starting transfers between devices: none -> 22.7 us  [pairwise_exchange(): outs.append(lax.ppermute(sent, axis, [(i, i ^ step) for i in range(size)]))]
    unnamed x11 -> x27, local copies, waits for them, and re-layouts: 2.27 us -> 17.4 us
    all_to_all x1 -> x0, starting transfers between devices: 6.03 us -> none  [per_device(): lax.all_to_all(out_grad, 'expert', split_axis=0, concat_axis=0, tiled=True)]
    gather x0 -> x1, local copies, waits for them, and re-layouts: none -> 5.35 us  [pairwise_exchange(): tiles = jnp.stack(outs)[index ^ jnp.arange(size)]]
  transfers between devices with their start and end apart: 7 -> 21, of which waited for: 5 -> 14; matrix products, arithmetic and copies ran while one was open for 12% -> 12% of each run, Pallas kernels for 0% -> 0%
where the time goes in v1:
time: 448 us; the launch traced here: 447 us
  waiting for transfers between devices  170 us (38%)
  blocking collectives  110 us (25%)
  local copies, waits for them, and re-layouts  69.6 us (16%)
  starting transfers between devices  39.8 us (9%)
  matrix products  24.4 us (5%)
  other arithmetic  19.9 us (4%)
  between operations  14 us (3%)
    all_to_all x1, blocking collectives, per_device(): lax.all_to_all(send_x, 'expert', split_axis=0, concat_axis=0, tiled=True)  110 us
    ppermute x15, waiting for transfers between devices, pairwise_exchange(): outs.append(lax.ppermute(sent, axis, [(i, i ^ step) for i in range(size)]))  78.1 us
    all_gather x1, waiting for transfers between devices, per_device(): lax.all_gather(w_gate[0], 'dp', axis=0, tiled=True)  27.6 us
    all_gather x1, waiting for transfers between devices, per_device(): lax.all_gather(w_up[0], 'dp', axis=0, tiled=True)  23.7 us
    ppermute x15, starting transfers between devices, pairwise_exchange(): outs.append(lax.ppermute(sent, axis, [(i, i ^ step) for i in range(size)]))  22.7 us
    all_gather x1, waiting for transfers between devices, per_device(): lax.all_gather(w_down[0], 'dp', axis=1, tiled=True)  22.4 us
    unnamed x27, local copies, waits for them, and re-layouts  17.4 us
    all_to_all x1, waiting for transfers between devices, per_device(): lax.all_to_all(send_g, 'expert', split_axis=0, concat_axis=0, tiled=True)  16.1 us
  transfers between devices with their start and end apart: 21, of which 14 were waited for; matrix products, arithmetic and copies ran while one was open for 12% of the time, Pallas kernels for 0%

profile of v1, /device:TPU:11, one launch (start us, length us, event | category | flops | bytes accessed | tf_op | source)
XLA Modules:
  0.0 447.4 jit_solution(5916201725483968552)
XLA Ops:
  7.2 0.8 copy.19
  8.2 0.7 broadcast_multiply_fusion
  8.9 4.5 %reduce-window.6 = s32[16,8,128]{2,1,0:T(8,128)S(1)} reduce-window(s32[16,8,128]{2,1,0:T(8,128)S(1)} %fusion.18, s32[]{:T(128)} %constant.36.clone.1), window={size=1x1x128 pad=0_0x0_0x127_0}, to_apply=%region_0.0 | reduce-window | flops 2080768 | bytes 131076 | tf_op jit(solution)/shard_map/reduce-window
  14.1 4.3 scatter_custom_fusion
  18.5 0.8 copy.23
  19.4 7.3 %gather_fusion = bf16[1152]{0:T(1024)(128)(2,1)S(1)} fusion(bf16[1024]{0:T(1024)(128)(2,1)S(1)} %reshape.150, s32[2048]{0:T(1024)S(1)} %get-tuple-element.30), kind=kCustom, calls=%fused_computation.2 | custom fusion | bytes 9216 | tf_op jit(solution)/shard_map/jit(_take)/gather | solution.py:51
  26.7 0.7 select_n.128
  27.4 6.5 %all-to-all-start = ((bf16[16,1,72]{2,1,0:T(2,128)(2,1)}), bf16[16,1,72]{2,1,0:T(2,128)(2,1)S(1)}, u32[]{:S(2)}, u32[]{:S(2)}) async-start(bf16[16,1,72]{2,1,0:T(2,128)(2,1)} %select_n.128), calls=%async_computation | async-start | bytes 16384 | tf_op jit(solution)/shard_map/all_to_all | solution.py:84
  33.9 5.9 %gather_fusion.4 = bf16[1152,2048]{1,0:T(8,128)(2,1)} fusion(bf16[128,2048]{1,0:T(8,128)(2,1)S(1)} %copy-done, s32[2048]{0:T(1024)S(1)} %get-tuple-element.29), kind=kCustom, calls=%fused_computation.clone | custom fusion | bytes 9441792 | tf_op jit(solution)/shard_map/jit(_take)/gather | solution.py:50
  39.8 6.0 %gather_fusion.5 = bf16[1152,2048]{1,0:T(8,128)(2,1)} fusion(bf16[128,2048]{1,0:T(8,128)(2,1)S(1)} %copy-done.2, s32[2048]{0:T(1024)S(1)} %get-tuple-element.29), kind=kCustom, calls=%fused_computation.1.clone | custom fusion | bytes 9441792 | tf_op jit(solution)/shard_map/jit(_take)/gather | solution.py:49
  45.8 8.5 %broadcast_select_fusion.1 = (bf16[1152,2048]{1,0:T(8,128)(2,1)}, bf16[1152,2048]{1,0:T(8,128)(2,1)}) fusion(bf16[1152,2048]{1,0:T(8,128)(2,1)} %gather_fusion.4, pred[1152]{0:T(1024)(128)(4,1)S(1)} %get-tuple-element.7, bf16[1152,2048]{1,0:T(8,128)(2,1)} %gather_fusion.5), kind=kLoop, calls=%fused_computation.10 | loop fusion | flops 4718592 | bytes 18875520 | tf_op jit(solution)/shard_map/jit(_take)/select_n | solution.py:50
  54.3 109.6 %all_to_all.22 = bf16[16,72,2048]{2,1,0:T(8,128)(2,1)} all-to-all(bf16[16,72,2048]{2,1,0:T(8,128)(2,1)} %bitcast.111), channel_id=1, replica_groups=mesh['dp'=2,'expert'=16] {'expert'}, dimensions={0} | all-to-all | bytes 9437184 | tf_op jit(solution)/shard_map/all_to_all | solution.py:82
  163.9 5.3 %all-to-all-start.1 = ((bf16[16,72,2048]{2,1,0:T(8,128)(2,1)}), bf16[16,72,2048]{2,1,0:T(8,128)(2,1)}, u32[]{:S(2)}, u32[]{:S(2)}) async-start(bf16[16,72,2048]{2,1,0:T(8,128)(2,1)} %bitcast.110), calls=%async_computation.1 | async-start | bytes 9437184 | tf_op jit(solution)/shard_map/all_to_all | solution.py:83
  169.9 0.7 all-gather.9.cloned.1.call-update
  171.6 27.6 %all-gather.11.cloned.1.call-done = bf16[1,2048,384]{2,1,0:T(8,128)(2,1)} async-done(((bf16[1,1024,384]{2,1,0:T(8,128)(2,1)}), bf16[1,2048,384]{2,1,0:T(8,128)(2,1)}) %all-gather.11.cloned.1.call-update) | async-done | bytes 1572880 | tf_op jit(solution)/shard_map/all_gather | solution.py:63
  199.2 5.1 %fusion.4 = f32[1152,384]{0,1:T(8,128)S(1)} fusion(bf16[1152,2048]{1,0:T(8,128)(2,1)} %bitcast.114, bf16[1,2048,384]{2,1,0:T(8,128)(2,1)} %all-gather.11.cloned.1.call-done), kind=kOutput, calls=%fused_computation.19 | convolution fusion | flops 1811939328 | bytes 8060928 | tf_op jit(solution)/shard_map/dot_general | solution.py:30
  204.3 23.7 %all-gather.9.cloned.1.call-done = bf16[1,2048,384]{2,1,0:T(8,128)(2,1)} async-done(((bf16[1,1024,384]{2,1,0:T(8,128)(2,1)}), bf16[1,2048,384]{2,1,0:T(8,128)(2,1)}) %all-gather.9.cloned.1.call-update) | async-done | bytes 1572880 | tf_op jit(solution)/shard_map/all_gather | solution.py:64
  228.0 6.3 %fusion.7 = f32[1152,384]{0,1:T(8,128)} fusion(bf16[1152,2048]{1,0:T(8,128)(2,1)} %bitcast.115, bf16[1,2048,384]{2,1,0:T(8,128)(2,1)} %all-gather.9.cloned.1.call-done), kind=kOutput, calls=%fused_computation.22 | convolution fusion | flops 1811939328 | bytes 8060928 | tf_op jit(solution)/shard_map/dot_general | solution.py:31
  234.3 22.4 %all-gather.7.cloned.1.call-done = bf16[1,384,2048]{2,1,0:T(8,128)(2,1)} async-done(((bf16[1,384,1024]{2,1,0:T(8,128)(2,1)}), bf16[1,384,2048]{2,1,0:T(8,128)(2,1)}) %all-gather.7.cloned.1.call-update) | async-done | bytes 1572880 | tf_op jit(solution)/shard_map/all_gather | solution.py:65
  256.7 16.1 %all-to-all-done.1 = bf16[16,72,2048]{2,1,0:T(8,128)(2,1)} async-done(((bf16[16,72,2048]{2,1,0:T(8,128)(2,1)}), bf16[16,72,2048]{2,1,0:T(8,128)(2,1)}, u32[]{:S(2)}, u32[]{:S(2)}) %all-to-all-start.1) | async-done | bytes 4718624 | tf_op jit(solution)/shard_map/all_to_all | solution.py:83
  272.9 5.8 %multiply_reduce_fusion = (bf16[1152]{0:T(1024)(128)(2,1)S(1)}, f32[1152,384]{0,1:T(8,128)S(1)}) fusion(f32[1152,384]{0,1:T(8,128)} %fusion.7, f32[1152,384]{0,1:T(8,128)S(1)} %fusion.4, bf16[1152,2048]{1,0:T(8,128)(2,1)} %bitcast.5, bf16[1,384,2048]{2,1,0:T(8,128)(2,1)} %all-gather.7.cloned.1.call-done), kind=kOutput, calls=%fused_computation.12 | convolution fusion | flops 1815034752 | bytes 11602176 | tf_op jit(solution)/shard_map/dot_general | solution.py:35
  278.7 3.0 fusion.2
  281.7 4.2 fusion
  285.9 1.6 dynamic-slice_bitcast_fusion
  288.3 5.0 %all-to-all-start.3 = ((bf16[16,1,72]{2,1,0:T(2,128)(2,1)}), bf16[16,1,72]{2,1,0:T(2,128)(2,1)S(1)}, u32[]{:S(2)}, u32[]{:S(2)}) async-start(bf16[16,1,72]{2,1,0:T(2,128)(2,1)} %convert_element_type.52), calls=%async_computation.3 | async-start | bytes 16384 | tf_op jit(solution)/shard_map/all_to_all | solution.py:98
  293.7 1.7 collective-permute-start.2
  295.8 1.2 collective-permute-start.4
  297.4 6.8 %gather_fusion.3 = bf16[1024]{0:T(1024)(128)(2,1)S(1)} fusion(bf16[1152]{0:T(1024)(128)(2,1)S(1)} %reshape.156, s32[1024]{0:T(1024)S(1)} %broadcast_clamp_fusion), kind=kCustom, calls=%fused_computation.5 | custom fusion | bytes 8192 | tf_op jit(solution)/shard_map/gather | solution.py:101
  304.9 2.1 collective-permute-start.5
  307.0 1.7 bitcast_dynamic-update-slice_fusion.14
  308.7 1.1 collective-permute-start.6
  309.8 1.7 bitcast_dynamic-update-slice_fusion.13
  311.5 1.5 collective-permute-start.7
  313.0 1.7 bitcast_dynamic-update-slice_fusion.12
  314.7 1.0 collective-permute-start.8
  315.7 1.7 bitcast_dynamic-update-slice_fusion.11
  317.4 1.4 collective-permute-start.9
  318.8 1.7 bitcast_dynamic-update-slice_fusion.10
  320.5 4.3 collective-permute-done.5
  324.8 5.2 %collective-permute-start.10 = (bf16[1,72,2048]{2,1,0:T(8,128)(2,1)S(1)}, bf16[1,72,2048]{2,1,0:T(8,128)(2,1)S(1)}, u32[]{:S(2)}, u32[]{:S(2)}) collective-permute-start(bf16[1,72,2048]{2,1,0:T(8,128)(2,1)S(1)} %get-tuple-element.13), channel_id=1, source_target_pairs={{0,11},{1,10},{2,9},{3,8},{4,15},{5,14},{6,13},{7,12},{8,3},{9,2},... | collective-permute-start | bytes 884744 | tf_op jit(solution)/shard_map/ppermute | solution.py:24
  330.1 0.8 bitcast_dynamic-update-slice_fusion.9
  331.2 1.5 collective-permute-start.11
  332.7 0.7 bitcast_dynamic-update-slice_fusion.8
  333.5 0.8 collective-permute-start.12
  334.2 0.7 bitcast_dynamic-update-slice_fusion.7
  334.9 28.9 %collective-permute-done.8 = bf16[1,72,2048]{2,1,0:T(8,128)(2,1)S(1)} collective-permute-done((bf16[1,72,2048]{2,1,0:T(8,128)(2,1)S(1)}, bf16[1,72,2048]{2,1,0:T(8,128)(2,1)S(1)}, u32[]{:S(2)}, u32[]{:S(2)}) %collective-permute-start.8) | collective-permute-done | bytes 294944 | tf_op jit(solution)/shard_map/ppermute | solution.py:24
  363.9 2.1 collective-permute-start.13
  366.0 0.7 bitcast_dynamic-update-slice_fusion.6
  366.7 9.8 %collective-permute-done.9 = bf16[1,72,2048]{2,1,0:T(8,128)(2,1)S(1)} collective-permute-done((bf16[1,72,2048]{2,1,0:T(8,128)(2,1)S(1)}, bf16[1,72,2048]{2,1,0:T(8,128)(2,1)S(1)}, u32[]{:S(2)}, u32[]{:S(2)}) %collective-permute-start.9) | collective-permute-done | bytes 294944 | tf_op jit(solution)/shard_map/ppermute | solution.py:24
  376.5 2.2 collective-permute-start.14
  378.7 0.7 bitcast_dynamic-update-slice_fusion.5
  379.4 3.3 collective-permute-done.10
  382.7 0.7 bitcast_dynamic-update-slice_fusion.4
  383.4 13.6 %collective-permute-done.11 = bf16[1,72,2048]{2,1,0:T(8,128)(2,1)S(1)} collective-permute-done((bf16[1,72,2048]{2,1,0:T(8,128)(2,1)S(1)}, bf16[1,72,2048]{2,1,0:T(8,128)(2,1)S(1)}, u32[]{:S(2)}, u32[]{:S(2)}) %collective-permute-start.11) | collective-permute-done | bytes 294944 | tf_op jit(solution)/shard_map/ppermute | solution.py:24
  397.0 0.7 bitcast_dynamic-update-slice_fusion.3
  397.7 5.6 %collective-permute-done.12 = bf16[1,72,2048]{2,1,0:T(8,128)(2,1)S(1)} collective-permute-done((bf16[1,72,2048]{2,1,0:T(8,128)(2,1)S(1)}, bf16[1,72,2048]{2,1,0:T(8,128)(2,1)S(1)}, u32[]{:S(2)}, u32[]{:S(2)}) %collective-permute-start.12) | collective-permute-done | bytes 294944 | tf_op jit(solution)/shard_map/ppermute | solution.py:24
  403.4 0.7 bitcast_dynamic-update-slice_fusion.2
  404.1 6.7 %collective-permute-done.13 = bf16[1,72,2048]{2,1,0:T(8,128)(2,1)S(1)} collective-permute-done((bf16[1,72,2048]{2,1,0:T(8,128)(2,1)S(1)}, bf16[1,72,2048]{2,1,0:T(8,128)(2,1)S(1)}, u32[]{:S(2)}, u32[]{:S(2)}) %collective-permute-start.13) | collective-permute-done | bytes 294944 | tf_op jit(solution)/shard_map/ppermute | solution.py:24
  410.8 0.7 bitcast_dynamic-update-slice_fusion.1
  411.5 5.6 %collective-permute-done.14 = bf16[1,72,2048]{2,1,0:T(8,128)(2,1)S(1)} collective-permute-done((bf16[1,72,2048]{2,1,0:T(8,128)(2,1)S(1)}, bf16[1,72,2048]{2,1,0:T(8,128)(2,1)S(1)}, u32[]{:S(2)}, u32[]{:S(2)}) %collective-permute-start.14) | collective-permute-done | bytes 294944 | tf_op jit(solution)/shard_map/ppermute | solution.py:24
  417.1 0.7 bitcast_dynamic-update-slice_fusion
  417.8 5.4 %gather_fusion.1 = bf16[16,72,2048]{2,1,0:T(8,128)(2,1)} fusion(bf16[16,72,2048]{2,1,0:T(8,128)(2,1)} %bitcast.113, s32[1024]{0:T(1024)S(1)} %pad_clamp_fusion.2), kind=kCustom, calls=%fused_computation.3 | custom fusion | bytes 9437248 | tf_op jit(solution)/shard_map/gather | solution.py:25
  423.2 11.8 %gather_fusion.2 = bf16[1024,2048]{1,0:T(8,128)(2,1)} fusion(bf16[1152,2048]{1,0:T(8,128)(2,1)} %bitcast.109, s32[1024]{0:T(1024)S(1)} %broadcast_clamp_fusion), kind=kCustom, calls=%fused_computation.4 | custom fusion | bytes 8392704 | tf_op jit(solution)/shard_map/gather | solution.py:100
  435.0 5.9 %bitcast_reduce_fusion = bf16[128,2048]{1,0:T(8,128)(2,1)} fusion(bf16[1024,2048]{1,0:T(8,128)(2,1)} %gather_fusion.2), kind=kLoop, calls=%fused_computation.11 | loop fusion | flops 1835008 | bytes 4718592 | tf_op jit(solution)/shard_map/reduce_sum | solution.py:103
  (56 shorter events, 5.5 us)
Async XLA Ops:
  7.2 26.7 %copy-start = (bf16[128,2048]{1,0:T(8,128)(2,1)S(1)}, bf16[128,2048]{1,0:T(8,128)(2,1)}, u32[]{:S(2)}) copy-start(bf16[128,2048]{1,0:T(8,128)(2,1)} %param.10) | copy-start | bytes 1572868
  27.4 27.0 %all-to-all-start = ((bf16[16,1,72]{2,1,0:T(2,128)(2,1)}), bf16[16,1,72]{2,1,0:T(2,128)(2,1)S(1)}, u32[]{:S(2)}, u32[]{:S(2)}) async-start(bf16[16,1,72]{2,1,0:T(2,128)(2,1)} %select_n.128), calls=%async_computation | async-start | bytes 16384 | tf_op jit(solution)/shard_map/all_to_all | solution.py:84
  33.9 5.9 %copy-start.2 = (bf16[128,2048]{1,0:T(8,128)(2,1)S(1)}, bf16[128,2048]{1,0:T(8,128)(2,1)}, u32[]{:S(2)}) copy-start(bf16[128,2048]{1,0:T(8,128)(2,1)} %param.9) | copy-start | bytes 1572868
  163.9 109.0 %all-to-all-start.1 = ((bf16[16,72,2048]{2,1,0:T(8,128)(2,1)}), bf16[16,72,2048]{2,1,0:T(8,128)(2,1)}, u32[]{:S(2)}, u32[]{:S(2)}) async-start(bf16[16,72,2048]{2,1,0:T(8,128)(2,1)} %bitcast.110), calls=%async_computation.1 | async-start | bytes 9437184 | tf_op jit(solution)/shard_map/all_to_all | solution.py:83
  169.2 30.0 %all-gather.11.cloned.1.call-start = ((), (), s32[]{:S(2)}) async-start(), calls=%async_computation.6 | async-start | bytes 2359296 | tf_op jit(solution)/shard_map/all_gather | solution.py:63
  169.9 58.1 %all-gather.9.cloned.1.call-start = ((), (), s32[]{:S(2)}) async-start(), calls=%async_computation.5 | async-start | bytes 2359296 | tf_op jit(solution)/shard_map/all_gather | solution.py:64
  170.6 86.1 %all-gather.7.cloned.1.call-start = ((), (), s32[]{:S(2)}) async-start(), calls=%async_computation.4 | async-start | bytes 2359296 | tf_op jit(solution)/shard_map/all_gather | solution.py:65
  272.9 5.8 %copy-start.3 = (f32[1152,384]{0,1:T(8,128)S(1)}, f32[1152,384]{0,1:T(8,128)}, u32[]{:S(2)}) copy-start(f32[1152,384]{0,1:T(8,128)} %fusion.7) | copy-start | bytes 5308420
  272.9 5.8 %copy-start.4 = (bf16[1,2048,384]{2,1,0:T(8,128)(2,1)S(1)}, bf16[1,2048,384]{2,1,0:T(8,128)(2,1)}, u32[]{:S(2)}) copy-start(bf16[1,2048,384]{2,1,0:T(8,128)(2,1)} %all-gather.11.cloned.1.call-done) | copy-start | bytes 4718596
  287.5 17.4 %collective-permute-start = (bf16[1,72,2048]{2,1,0:T(8,128)(2,1)}, bf16[1,72,2048]{2,1,0:T(8,128)(2,1)}, u32[]{:S(2)}, u32[]{:S(2)}) collective-permute-start(bf16[1,72,2048]{2,1,0:T(8,128)(2,1)} %get-tuple-element.23), channel_id=1, source_target_pairs={{0,1},{1,0},{2,3},{3,2},{4,5},{5,4},{6,7},{7,6},{8,9},{9,8},{10,11... | collective-permute-start | bytes 884744 | tf_op jit(solution)/shard_map/ppermute | solution.py:24
  288.3 8.9 %all-to-all-start.3 = ((bf16[16,1,72]{2,1,0:T(2,128)(2,1)}), bf16[16,1,72]{2,1,0:T(2,128)(2,1)S(1)}, u32[]{:S(2)}, u32[]{:S(2)}) async-start(bf16[16,1,72]{2,1,0:T(2,128)(2,1)} %convert_element_type.52), calls=%async_computation.3 | async-start | bytes 16384 | tf_op jit(solution)/shard_map/all_to_all | solution.py:98
  293.4 15.3 %collective-permute-start.1 = (bf16[1,72,2048]{2,1,0:T(8,128)(2,1)}, bf16[1,72,2048]{2,1,0:T(8,128)(2,1)}, u32[]{:S(2)}, u32[]{:S(2)}) collective-permute-start(bf16[1,72,2048]{2,1,0:T(8,128)(2,1)} %get-tuple-element.22), channel_id=1, source_target_pairs={{0,2},{1,3},{2,0},{3,1},{4,6},{5,7},{6,4},{7,5},{8,10},{9,11},{10,... | collective-permute-start | bytes 884744 | tf_op jit(solution)/shard_map/ppermute | solution.py:24
  293.7 17.8 %collective-permute-start.2 = (bf16[1,72,2048]{2,1,0:T(8,128)(2,1)}, bf16[1,72,2048]{2,1,0:T(8,128)(2,1)}, u32[]{:S(2)}, u32[]{:S(2)}) collective-permute-start(bf16[1,72,2048]{2,1,0:T(8,128)(2,1)} %get-tuple-element.21), channel_id=1, source_target_pairs={{0,3},{1,2},{2,1},{3,0},{4,7},{5,6},{6,5},{7,4},{8,11},{9,10},{10,... | collective-permute-start | bytes 884744 | tf_op jit(solution)/shard_map/ppermute | solution.py:24
  295.5 19.3 %collective-permute-start.3 = (bf16[1,72,2048]{2,1,0:T(8,128)(2,1)}, bf16[1,72,2048]{2,1,0:T(8,128)(2,1)}, u32[]{:S(2)}, u32[]{:S(2)}) collective-permute-start(bf16[1,72,2048]{2,1,0:T(8,128)(2,1)} %get-tuple-element.20), channel_id=1, source_target_pairs={{0,4},{1,5},{2,6},{3,7},{4,0},{5,1},{6,2},{7,3},{8,12},{9,13},{10,... | collective-permute-start | bytes 884744 | tf_op jit(solution)/shard_map/ppermute | solution.py:24
  295.8 21.6 %collective-permute-start.4 = (bf16[1,72,2048]{2,1,0:T(8,128)(2,1)S(1)}, bf16[1,72,2048]{2,1,0:T(8,128)(2,1)}, u32[]{:S(2)}, u32[]{:S(2)}) collective-permute-start(bf16[1,72,2048]{2,1,0:T(8,128)(2,1)S(1)} %get-tuple-element.19), channel_id=1, source_target_pairs={{0,5},{1,4},{2,7},{3,6},{4,1},{5,0},{6,3},{7,2},{8,13},{9,12},{10,... | collective-permute-start | bytes 884744 | tf_op jit(solution)/shard_map/ppermute | solution.py:24
  304.9 19.9 %collective-permute-start.5 = (bf16[1,72,2048]{2,1,0:T(8,128)(2,1)S(1)}, bf16[1,72,2048]{2,1,0:T(8,128)(2,1)S(1)}, u32[]{:S(2)}, u32[]{:S(2)}) collective-permute-start(bf16[1,72,2048]{2,1,0:T(8,128)(2,1)S(1)} %get-tuple-element.18), channel_id=1, source_target_pairs={{0,6},{1,7},{2,4},{3,5},{4,2},{5,3},{6,0},{7,1},{8,14},{9,15},{10,... | collective-permute-start | bytes 884744 | tf_op jit(solution)/shard_map/ppermute | solution.py:24
  308.7 22.5 %collective-permute-start.6 = (bf16[1,72,2048]{2,1,0:T(8,128)(2,1)S(1)}, bf16[1,72,2048]{2,1,0:T(8,128)(2,1)S(1)}, u32[]{:S(2)}, u32[]{:S(2)}) collective-permute-start(bf16[1,72,2048]{2,1,0:T(8,128)(2,1)S(1)} %get-tuple-element.17), channel_id=1, source_target_pairs={{0,7},{1,6},{2,5},{3,4},{4,3},{5,2},{6,1},{7,0},{8,15},{9,14},{10,... | collective-permute-start | bytes 884744 | tf_op jit(solution)/shard_map/ppermute | solution.py:24
  311.5 22.0 %collective-permute-start.7 = (bf16[1,72,2048]{2,1,0:T(8,128)(2,1)S(1)}, bf16[1,72,2048]{2,1,0:T(8,128)(2,1)S(1)}, u32[]{:S(2)}, u32[]{:S(2)}) collective-permute-start(bf16[1,72,2048]{2,1,0:T(8,128)(2,1)S(1)} %get-tuple-element.16), channel_id=1, source_target_pairs={{0,8},{1,9},{2,10},{3,11},{4,12},{5,13},{6,14},{7,15},{8,0},{9,1},... | collective-permute-start | bytes 884744 | tf_op jit(solution)/shard_map/ppermute | solution.py:24
  314.7 49.1 %collective-permute-start.8 = (bf16[1,72,2048]{2,1,0:T(8,128)(2,1)S(1)}, bf16[1,72,2048]{2,1,0:T(8,128)(2,1)S(1)}, u32[]{:S(2)}, u32[]{:S(2)}) collective-permute-start(bf16[1,72,2048]{2,1,0:T(8,128)(2,1)S(1)} %get-tuple-element.15), channel_id=1, source_target_pairs={{0,9},{1,8},{2,11},{3,10},{4,13},{5,12},{6,15},{7,14},{8,1},{9,0},... | collective-permute-start | bytes 884744 | tf_op jit(solution)/shard_map/ppermute | solution.py:24
  317.4 59.1 %collective-permute-start.9 = (bf16[1,72,2048]{2,1,0:T(8,128)(2,1)S(1)}, bf16[1,72,2048]{2,1,0:T(8,128)(2,1)S(1)}, u32[]{:S(2)}, u32[]{:S(2)}) collective-permute-start(bf16[1,72,2048]{2,1,0:T(8,128)(2,1)S(1)} %get-tuple-element.14), channel_id=1, source_target_pairs={{0,10},{1,11},{2,8},{3,9},{4,14},{5,15},{6,12},{7,13},{8,2},{9,3},... | collective-permute-start | bytes 884744 | tf_op jit(solution)/shard_map/ppermute | solution.py:24
  324.8 57.8 %collective-permute-start.10 = (bf16[1,72,2048]{2,1,0:T(8,128)(2,1)S(1)}, bf16[1,72,2048]{2,1,0:T(8,128)(2,1)S(1)}, u32[]{:S(2)}, u32[]{:S(2)}) collective-permute-start(bf16[1,72,2048]{2,1,0:T(8,128)(2,1)S(1)} %get-tuple-element.13), channel_id=1, source_target_pairs={{0,11},{1,10},{2,9},{3,8},{4,15},{5,14},{6,13},{7,12},{8,3},{9,2},... | collective-permute-start | bytes 884744 | tf_op jit(solution)/shard_map/ppermute | solution.py:24
  331.2 65.8 %collective-permute-start.11 = (bf16[1,72,2048]{2,1,0:T(8,128)(2,1)S(1)}, bf16[1,72,2048]{2,1,0:T(8,128)(2,1)S(1)}, u32[]{:S(2)}, u32[]{:S(2)}) collective-permute-start(bf16[1,72,2048]{2,1,0:T(8,128)(2,1)S(1)} %get-tuple-element.12), channel_id=1, source_target_pairs={{0,12},{1,13},{2,14},{3,15},{4,8},{5,9},{6,10},{7,11},{8,4},{9,5},... | collective-permute-start | bytes 884744 | tf_op jit(solution)/shard_map/ppermute | solution.py:24
  333.5 69.9 %collective-permute-start.12 = (bf16[1,72,2048]{2,1,0:T(8,128)(2,1)S(1)}, bf16[1,72,2048]{2,1,0:T(8,128)(2,1)S(1)}, u32[]{:S(2)}, u32[]{:S(2)}) collective-permute-start(bf16[1,72,2048]{2,1,0:T(8,128)(2,1)S(1)} %get-tuple-element.11), channel_id=1, source_target_pairs={{0,13},{1,12},{2,15},{3,14},{4,9},{5,8},{6,11},{7,10},{8,5},{9,4},... | collective-permute-start | bytes 884744 | tf_op jit(solution)/shard_map/ppermute | solution.py:24
  363.9 46.9 %collective-permute-start.13 = (bf16[1,72,2048]{2,1,0:T(8,128)(2,1)S(1)}, bf16[1,72,2048]{2,1,0:T(8,128)(2,1)S(1)}, u32[]{:S(2)}, u32[]{:S(2)}) collective-permute-start(bf16[1,72,2048]{2,1,0:T(8,128)(2,1)S(1)} %get-tuple-element.10), channel_id=1, source_target_pairs={{0,14},{1,15},{2,12},{3,13},{4,10},{5,11},{6,8},{7,9},{8,6},{9,7},... | collective-permute-start | bytes 884744 | tf_op jit(solution)/shard_map/ppermute | solution.py:24
  376.5 40.6 %collective-permute-start.14 = (bf16[1,72,2048]{2,1,0:T(8,128)(2,1)S(1)}, bf16[1,72,2048]{2,1,0:T(8,128)(2,1)S(1)}, u32[]{:S(2)}, u32[]{:S(2)}) collective-permute-start(bf16[1,72,2048]{2,1,0:T(8,128)(2,1)S(1)} %get-tuple-element.9), channel_id=1, source_target_pairs={{0,15},{1,14},{2,13},{3,12},{4,11},{5,10},{6,9},{7,8},{8,7},{9,6},... | collective-permute-start | bytes 884744 | tf_op jit(solution)/shard_map/ppermute | solution.py:24
  423.2 17.7 %copy-start.1 = (bf16[128,2048]{1,0:T(8,128)(2,1)S(1)}, bf16[128,2048]{1,0:T(8,128)(2,1)}, u32[]{:S(2)}) copy-start(bf16[128,2048]{1,0:T(8,128)(2,1)} %param.10) | copy-start | bytes 1572868
Sparse Core Ops, SparseCore 0:
  171.5 27.6 all-gather.10
  200.7 27.1 all-gather.8
  229.5 27.1 all-gather.6
